TPU v7x, 32 devices: a whole 2x2x4 slice. The times are simulated.
32 devices in a mesh: groups: 2 (over x), pool: 2 (over core), tensor: 8 (over z, y).
Axes of the slice: x: 2, y: 2, z: 4, core: 2. Of those that a mesh axis runs over, the one named last changes fastest.
Arguments:
- hidden: bfloat16 [64, 5120], P(('groups', 'pool', 'tensor')), parts along dimension 0, may hold values from -1.5 to 1.5
- input_gain: float32 [5120], replicated, may hold values from 0.1 to 1.9
- query_weight: bfloat16 [5120, 4096], P(None, ('pool', 'tensor')), may hold values from -0.078125 to 0.078125
- key_weight: bfloat16 [5120, 512], P(None, ('pool', 'tensor')), may hold values from -0.078125 to 0.078125
- value_weight: bfloat16 [5120, 512], P(None, ('pool', 'tensor')), may hold values from -0.078125 to 0.078125
- query_gain: float32 [128], replicated, may hold values from 2 to 6
- key_gain: float32 [128], replicated, may hold values from 1 to 4
- output_weight: bfloat16 [4096, 5120], P(('pool', 'tensor')), may hold values from -0.09375 to 0.09375
- post_gain: float32 [5120], replicated, may hold values from 0.1 to 1.9
- gate_weight: bfloat16 [5120, 12800], P(None, ('pool', 'tensor')), may hold values from -0.078125 to 0.078125
- up_weight: bfloat16 [5120, 12800], P(None, ('pool', 'tensor')), may hold values from -0.078125 to 0.078125
- down_weight: bfloat16 [12800, 5120], P(('pool', 'tensor')), may hold values from -0.0546875 to 0.0546875
- key_cache: bfloat16 [65536, 512], P(('groups', 'pool', 'tensor')), parts along dimension 0, may hold values from -45 to 45
- value_cache: bfloat16 [65536, 512], P(('groups', 'pool', 'tensor')), parts along dimension 0, may hold values from -6 to 6
- lengths: int32 [64], P('groups'), parts along dimension 0, may hold values from 128 to 2048, as said below
- request_slot: int32 [64], P('groups'), parts along dimension 0, may hold values from 0 to 63, as said below
Outputs:
- mixed: bfloat16 [64, 5120], P(('groups', 'pool', 'tensor')), parts along dimension 0
- final: bfloat16 [64, 5120], P(('groups', 'pool', 'tensor')), parts along dimension 0
There are 2 independent parts, one for each index of `groups`. A program takes and returns all parts, laid end to end along the dimension named above; an argument that names none is the same for every part. Nothing has to cross between parts.
Inputs may be any that keep to these rules, and one draw needn't show every extreme that they name: `request_slot`: each owner holds at most 4 requests and some owner holds exactly 4; no two requests share a slot. The lengths of one owner's requests sum to at most 2048; some request has exactly 2048 and some exactly 128.
All inputs are finite; a program needn't handle non-finite values.
Results may differ from a plain program's by a relative error of at most 0.03.
The roundings to bfloat16 on the way count: a program that leaves them out, or rounds other values in their place, can miss the bound.
Values may be sent and summed in bfloat16 or wider, within the bound.
A program may use at most 64 MiB of HBM per device.

v0:
```python
import math

import jax
import jax.numpy as jnp
from jax import lax
from jax.sharding import PartitionSpec as P

SLOTS = 4


eps = 1e-06
theta = 1000000.0


def rms_scale(values, scales):
    values = values.astype(jnp.float32)
    return values * lax.rsqrt(jnp.mean(values * values, axis=-1, keepdims=True) + eps) * scales


def rotate(values, position):
    half_width = values.shape[-1] // 2
    frequency = theta ** (-jnp.arange(half_width, dtype=jnp.float32) * 2.0 / values.shape[-1])
    angles = position * frequency
    cosine = jnp.cos(angles)
    sine_part = jnp.sin(angles)
    front_half = values[..., :half_width]
    back_half = values[..., half_width:]
    return jnp.concatenate(
        [front_half * cosine - back_half * sine_part, back_half * cosine + front_half * sine_part],
        axis=-1,
    )


def on_device(
    hidden,
    input_gain,
    query_weight,
    key_weight,
    value_weight,
    query_gain,
    key_gain,
    output_weight,
    post_gain,
    gate_weight,
    up_weight,
    down_weight,
    key_cache,
    value_cache,
    lengths,
    request_slot,
):
    devices = lax.axis_size(("pool", "tensor"))
    device_index = lax.axis_index(("pool", "tensor"))
    local_rows = hidden.shape[0]
    query_cols = query_weight.shape[1]
    key_cols = key_weight.shape[1]
    width_sent = query_cols + 2 * key_cols
    head_dim = query_gain.shape[0]
    slot_count = SLOTS
    head_count = devices * query_cols // head_dim
    kv_count = devices * key_cols // head_dim
    group_size = head_count // kv_count
    normed = rms_scale(hidden, input_gain).astype(jnp.bfloat16)
    shard_rows = lax.all_gather(normed, ("pool", "tensor"), axis=0, tiled=True)
    query_part = jnp.dot(shard_rows, query_weight, preferred_element_type=jnp.float32)
    key_part = jnp.dot(shard_rows, key_weight, preferred_element_type=jnp.float32)
    value_part = jnp.dot(shard_rows, value_weight, preferred_element_type=jnp.float32)
    projected = jnp.concatenate([query_part, key_part, value_part], axis=1).astype(jnp.bfloat16)
    outgoing = (
        jnp.zeros((devices * slot_count, width_sent), jnp.bfloat16).at[request_slot].set(projected)
    )
    outgoing = outgoing.reshape(devices, slot_count, width_sent)
    arrived = lax.all_to_all(
        outgoing, ("pool", "tensor"), split_axis=0, concat_axis=2, tiled=True
    ).reshape(slot_count, devices, width_sent)
    query_full = arrived[:, :, :query_cols].reshape(slot_count, head_count, head_dim)
    key_full = arrived[:, :, query_cols : query_cols + key_cols].reshape(
        slot_count, kv_count, head_dim
    )
    value_new = arrived[:, :, query_cols + key_cols :].reshape(slot_count, kv_count, head_dim)
    slot_ids = device_index * slot_count + jnp.arange(slot_count, dtype=jnp.int32)
    matches = request_slot[None, :] == slot_ids[:, None]
    slot_length = jnp.sum(jnp.where(matches, lengths[None, :], 0), axis=1)
    owner_of = request_slot // slot_count
    within = request_slot % slot_count
    earlier = (owner_of[None, :] == device_index) & (
        within[None, :] < jnp.arange(slot_count, dtype=jnp.int32)[:, None]
    )
    slot_offset = jnp.sum(jnp.where(earlier, lengths[None, :], 0), axis=1)
    position = slot_length.astype(jnp.float32)[:, None, None]
    query_heads = rotate(rms_scale(query_full, query_gain), position).astype(jnp.bfloat16)
    query_heads = query_heads.reshape(slot_count, kv_count, group_size, head_dim)
    key_new = rotate(rms_scale(key_full, key_gain), position).astype(jnp.bfloat16)
    pool_tokens = key_cache.shape[0]
    cached_keys = key_cache.reshape(pool_tokens, kv_count, head_dim)
    cached_values = value_cache.reshape(pool_tokens, kv_count, head_dim)
    scale_factor = 1.0 / math.sqrt(head_dim)
    scores = (
        jnp.einsum("skgd,tkd->skgt", query_heads, cached_keys, preferred_element_type=jnp.float32)
        * scale_factor
    )
    own_score = (
        jnp.einsum("skgd,skd->skg", query_heads, key_new, preferred_element_type=jnp.float32)
        * scale_factor
    )
    token_pos = jnp.arange(pool_tokens, dtype=jnp.int32)
    inside = (token_pos[None, :] >= slot_offset[:, None]) & (
        token_pos[None, :] < (slot_offset + slot_length)[:, None]
    )
    inside = inside[:, None, None, :]
    largest = jnp.maximum(jnp.max(jnp.where(inside, scores, -1e30), axis=3), own_score)
    weights = jnp.where(inside, jnp.exp(scores - largest[..., None]), 0.0)
    own_weight = jnp.exp(own_score - largest)
    denominator = jnp.sum(weights, axis=3) + own_weight
    summed = jnp.einsum(
        "skgt,tkd->skgd",
        weights.astype(jnp.bfloat16),
        cached_values,
        preferred_element_type=jnp.float32,
    )
    own_low = own_weight.astype(jnp.bfloat16).astype(jnp.float32)
    summed = summed + own_low[..., None] * value_new.astype(jnp.float32)[:, :, None, :]
    head_out = (
        (summed / denominator[..., None])
        .astype(jnp.bfloat16)
        .reshape(slot_count, devices, query_cols)
    )
    returned = lax.all_to_all(head_out, ("pool", "tensor"), split_axis=1, concat_axis=0, tiled=True)
    head_rows = returned.reshape(devices * slot_count, query_cols)[request_slot]
    partial_value = jnp.dot(head_rows, output_weight, preferred_element_type=jnp.float32)
    row_start = device_index * local_rows
    own_part = lax.dynamic_slice_in_dim(partial_value, row_start, local_rows, 0) + hidden.astype(
        jnp.float32
    )
    partial_value = lax.dynamic_update_slice_in_dim(partial_value, own_part, row_start, 0)
    totals = lax.psum(partial_value, ("pool", "tensor"))
    mixed_all = totals.astype(jnp.bfloat16)
    mixed_rows = lax.dynamic_slice_in_dim(mixed_all, row_start, local_rows, 0)
    post_normed = rms_scale(mixed_all, post_gain).astype(jnp.bfloat16)
    gate_part = jnp.dot(post_normed, gate_weight, preferred_element_type=jnp.float32)
    up_part = jnp.dot(post_normed, up_weight, preferred_element_type=jnp.float32)
    activated = (jax.nn.silu(gate_part) * up_part).astype(jnp.bfloat16)
    lowered = lax.psum_scatter(
        jnp.dot(activated, down_weight, preferred_element_type=jnp.float32),
        ("pool", "tensor"),
        scatter_dimension=0,
        tiled=True,
    )
    final_rows = (mixed_rows.astype(jnp.float32) + lowered).astype(jnp.bfloat16)
    return (mixed_rows, final_rows)


def solution(mesh):
    placed = (
        P(("groups", "pool", "tensor"), None),
        P(),
        P(None, ("pool", "tensor")),
        P(None, ("pool", "tensor")),
        P(None, ("pool", "tensor")),
        P(),
        P(),
        P(("pool", "tensor"), None),
        P(),
        P(None, ("pool", "tensor")),
        P(None, ("pool", "tensor")),
        P(("pool", "tensor"), None),
        P(("groups", "pool", "tensor"), None),
        P(("groups", "pool", "tensor"), None),
        P("groups"),
        P("groups"),
    )
    return jax.shard_map(
        on_device,
        mesh=mesh,
        in_specs=placed,
        out_specs=(P(("groups", "pool", "tensor"), None), P(("groups", "pool", "tensor"), None)),
        check_vma=False,
    )
```

profile of v0, /device:TPU:0, one launch (start us, length us, event | category | flops | bytes accessed | tf_op | source)
XLA Modules:
  0.0 270.1 jit_solution(12673101393724462071)
XLA Ops:
  7.2 1.0 fusion.37
  8.2 0.7 and_select_fusion
  8.9 0.8 fusion.53
  9.7 36.2 %all-gather = bf16[16,2,5120]{2,1,0:T(2,128)(2,1)S(1)} all-gather(bf16[1,2,5120]{2,1,0:T(2,128)(2,1)S(1)} %fusion.53), channel_id=1, replica_groups=mesh['groups'=2,'pool'=2,'tensor'=8] {'pool','tensor'}, dimensions={0}, use_global_device_ids=true | all-gather | bytes 348160 | tf_op jit(solution)/shard_map/all_gather | solution.py:64
  45.9 0.1 reshape.227
  46.0 1.2 convolution_convert_fusion.1
  47.2 1.2 convolution_convert_fusion.2
  48.4 2.3 convolution_convert_fusion
  50.7 0.8 scatter_custom_fusion
  51.5 0.7 reshape.199
  52.2 3.5 %all-to-all-start = ((bf16[16,4,320]{2,1,0:T(4,128)(2,1)}), bf16[16,4,320]{2,1,0:T(4,128)(2,1)S(1)}, u32[]{:S(2)}, u32[]{:S(2)}) async-start(bf16[16,4,320]{2,1,0:T(4,128)(2,1)} %reshape.199), calls=%async_computation | async-start | bytes 98304 | tf_op jit(solution)/shard_map/all_to_all | solution.py:73
  55.8 0.2 select_reduce_fusion.2
  56.1 0.1 multiply_cosine_fusion
  56.2 4.0 %reshape.201 = bf16[2048,4,128]{2,1,0:T(4,128)(2,1)} reshape(bf16[2048,512]{1,0:T(8,128)(2,1)} %param.28) | data formatting | bytes 4194304 | tf_op jit(solution)/shard_map/reshape | solution.py:95
  60.2 4.0 %reshape.202 = bf16[2048,4,128]{2,1,0:T(4,128)(2,1)} reshape(bf16[2048,512]{1,0:T(8,128)(2,1)} %param.29) | data formatting | bytes 4194304 | tf_op jit(solution)/shard_map/reshape | solution.py:96
  65.4 0.1 fusion.54
  65.5 2.5 select_reduce_fusion
  68.0 0.4 fusion.17
  68.4 0.7 fusion.14
  69.2 0.6 copy.78
  69.8 5.9 %all-to-all-start.1 = ((bf16[4,16,256]{2,0,1:T(4,128)(2,1)}), bf16[4,16,256]{2,0,1:T(4,128)(2,1)S(1)}, u32[]{:S(2)}, u32[]{:S(2)}) async-start(bf16[4,16,256]{2,0,1:T(4,128)(2,1)} %copy.78), calls=%async_computation.1 | async-start | bytes 65536 | tf_op jit(solution)/shard_map/all_to_all | solution.py:128
  75.8 6.5 %all-to-all-done.1 = bf16[4,16,256]{2,0,1:T(4,128)(2,1)S(1)} async-done(((bf16[4,16,256]{2,0,1:T(4,128)(2,1)}), bf16[4,16,256]{2,0,1:T(4,128)(2,1)S(1)}, u32[]{:S(2)}, u32[]{:S(2)}) %all-to-all-start.1) | async-done | bytes 32800 | tf_op jit(solution)/shard_map/all_to_all | solution.py:128
  82.3 0.6 gather_fusion
  82.9 1.4 fusion.63
  84.3 1.6 fusion.40
  85.9 66.3 %all-reduce.5 = bf16[32,5120]{1,0:T(8,128)(2,1)S(1)} all-reduce(f32[32,5120]{1,0:T(8,128)} %fusion.40), channel_id=1, replica_groups=mesh['groups'=2,'pool'=2,'tensor'=8] {'pool','tensor'}, use_global_device_ids=true, to_apply=%region_9.10 | all-reduce | flops 163840 | bytes 983040 | tf_op jit(solution)/shard_map/psum | solution.py:136
  152.2 0.2 fusion.20
  152.4 5.8 %fusion.34 = f32[32,800]{1,0:T(8,128)S(1)} fusion(bf16[5120,800]{0,1:T(8,128)(2,1)} %param.25, bf16[32,5120]{1,0:T(8,128)(2,1)S(1)} %all-reduce.5, f32[5120]{0:T(1024)S(1)} %copy-done.3, f32[32]{0:T(128)S(1)} %add_rsqrt_fusion.2), kind=kOutput, calls=%fused_computation.34 | convolution fusion | flops 262799360 | bytes 8642688 | tf_op jit(solution)/shard_map/dot_general | solution.py:140
  158.2 11.4 %fusion.19 = f32[32,5120]{1,0:T(8,128)} fusion(bf16[800,5120]{1,0:T(8,128)(2,1)} %param.27, bf16[5120,800]{0,1:T(8,128)(2,1)} %param.26, f32[32,800]{1,0:T(8,128)S(1)} %fusion.34, bf16[32,5120]{1,0:T(8,128)(2,1)S(1)} %all-reduce.5, f32[5120]{0:T(1024)S(1)} %copy-done.3, f32[32]{0:T(128)S(1)} %add_rsqrt_fusion.2), kind=kOutput, calls=%fused_computation.22 | convolution fusion | flops 525096960 | bytes 17490048 | tf_op jit(solution)/shard_map/dot_general | solution.py:144
  169.7 0.6 dynamic-slice
  170.9 90.8 %all-reduce.4.cloned.1.call-done = f32[32,5120]{1,0:T(8,128)} async-done(((f32[32,5120]{1,0:T(8,128)}), f32[32,5120]{1,0:T(8,128)}) %all-reduce.4.cloned.1.call-update) | async-done | bytes 655376
  261.7 1.6 fusion.41
  (54 shorter events, 1.5 us)
Async XLA Ops:
  7.2 75.7 %copy-start = (bf16[256,5120]{1,0:T(8,128)(2,1)S(1)}, bf16[256,5120]{1,0:T(8,128)(2,1)}, u32[]{:S(2)}) copy-start(bf16[256,5120]{1,0:T(8,128)(2,1)} %param.23) | copy-start | bytes 7864324
  45.9 9.8 %copy-start.6 = (s32[32]{0:T(128)S(1)}, s32[32]{0:T(128)}, u32[]{:S(2)}) copy-start(s32[32]{0:T(128)} %param.31) | copy-start | bytes 388
  45.9 9.9 %copy-start.5 = (s32[32]{0:T(128)S(1)}, s32[32]{0:T(128)}, u32[]{:S(2)}) copy-start(s32[32]{0:T(128)} %param.30) | copy-start | bytes 388
  52.2 12.0 %all-to-all-start = ((bf16[16,4,320]{2,1,0:T(4,128)(2,1)}), bf16[16,4,320]{2,1,0:T(4,128)(2,1)S(1)}, u32[]{:S(2)}, u32[]{:S(2)}) async-start(bf16[16,4,320]{2,1,0:T(4,128)(2,1)} %reshape.199), calls=%async_computation | async-start | bytes 98304 | tf_op jit(solution)/shard_map/all_to_all | solution.py:73
  60.2 4.7 %copy-start.4 = (f32[128]{0:T(128)S(1)}, f32[128]{0:T(128)}, u32[]{:S(2)}) copy-start(f32[128]{0:T(128)} %param.21) | copy-start | bytes 1540
  60.2 4.9 %copy-start.7 = (f32[128]{0:T(128)S(1)}, f32[128]{0:T(128)}, u32[]{:S(2)}) copy-start(f32[128]{0:T(128)} %param.22) | copy-start | bytes 1540
  64.9 3.5 %copy-start.1 = (bf16[2048,4,128]{2,1,0:T(4,128)(2,1)S(1)}, bf16[2048,4,128]{2,1,0:T(4,128)(2,1)}, u32[]{:S(2)}) copy-start(bf16[2048,4,128]{2,1,0:T(4,128)(2,1)} %reshape.202) | copy-start | bytes 6291460
  69.1 15.2 %copy-start.2 = (bf16[2,5120]{1,0:T(2,128)(2,1)S(1)}, bf16[2,5120]{1,0:T(2,128)(2,1)}, u32[]{:S(2)}) copy-start(bf16[2,5120]{1,0:T(2,128)(2,1)} %param.16) | copy-start | bytes 61444
  69.1 83.3 %copy-start.3 = (f32[5120]{0:T(1024)S(1)}, f32[5120]{0:T(1024)}, u32[]{:S(2)}) copy-start(f32[5120]{0:T(1024)} %param.24) | copy-start | bytes 61444
  69.8 12.5 %all-to-all-start.1 = ((bf16[4,16,256]{2,0,1:T(4,128)(2,1)}), bf16[4,16,256]{2,0,1:T(4,128)(2,1)S(1)}, u32[]{:S(2)}, u32[]{:S(2)}) async-start(bf16[4,16,256]{2,0,1:T(4,128)(2,1)} %copy.78), calls=%async_computation.1 | async-start | bytes 65536 | tf_op jit(solution)/shard_map/all_to_all | solution.py:128
  75.7 186.0 %all-reduce.4.cloned.1.call-start = ((), (), s32[]{:S(2)}) async-start(), calls=%async_computation.2 | async-start | bytes 1310720
  158.2 11.4 %copy-start.8 = (u32[32]{0:T(128)S(1)}, u32[32]{0:T(128)}, u32[]{:S(2)}) copy-start(u32[32]{0:T(128)} %constant.85) | copy-start | bytes 388
Sparse Core Ops, SparseCore 0:
  169.8 91.8 all-reduce.3
where the time goes:
time: 271 us; the launch traced here: 270 us
  blocking collectives  102 us (38%)
  waiting for transfers between devices  97.3 us (36%)
  matrix products  26.6 us (10%)
  between operations  15 us (6%)
  local copies, waits for them, and re-layouts  11 us (4%)
  starting transfers between devices  9.46 us (3%)
  other arithmetic  8.24 us (3%)
    unnamed x2, waiting for transfers between devices  90.8 us
    psum x1, blocking collectives, on_device(): totals = lax.psum(partial_value, ('pool', 'tensor'))  66.3 us
    all_gather x1, blocking collectives, on_device(): shard_rows = lax.all_gather(normed, ('pool', 'tensor'), axis=0, tiled=True)  36.2 us
    dot_general x1, matrix products, on_device(): jnp.dot(activated, down_weight, preferred_element_type=jnp.float32)  11.4 us
    all_to_all x1, waiting for transfers between devices, on_device(): lax.all_to_all(head_out, ('pool', 'tensor'), split_axis=1, concat_axis=0,...  6.5 us
    all_to_all x1, starting transfers between devices, on_device(): lax.all_to_all(head_out, ('pool', 'tensor'), split_axis=1, concat_axis=0,...  5.92 us
    dot_general x1, matrix products, on_device(): jnp.dot(post_normed, gate_weight, preferred_element_type=jnp.float32)  5.81 us
  transfers between devices with their start and end apart: 3, of which 2 were waited for; matrix products, arithmetic and copies ran while one was open for 3% of the time, Pallas kernels for 0%

commit v1 on v0

--- a/solution.py
+++ b/solution.py
@@ -1,8 +1,11 @@
+import functools
 import math
 
 import jax
 import jax.numpy as jnp
 from jax import lax
+from jax.experimental import pallas as pl
+from jax.experimental.pallas import tpu as pltpu
 from jax.sharding import PartitionSpec as P
 
 SLOTS = 4
@@ -150,6 +153,558 @@
     return (mixed_rows, final_rows)
 
 
+MESH = pl.DeviceIdType.MESH
+F32 = jnp.float32
+BF16 = jnp.bfloat16
+
+
+def step_kernel(
+    pool,
+    tensor,
+    hidden_ref,
+    input_gain_ref,
+    query_gain_ref,
+    key_gain_ref,
+    post_gain_ref,
+    length_ref,
+    slot_ref,
+    frequency_ref,
+    qw_hbm,
+    kw_hbm,
+    vw_hbm,
+    ow_hbm,
+    gw_hbm,
+    uw_hbm,
+    dw_hbm,
+    kc_hbm,
+    vc_hbm,
+    mixed_ref,
+    final_ref,
+    qw,
+    kw,
+    vw,
+    ow,
+    gw,
+    uw,
+    dw,
+    kc,
+    vc,
+    ag1,
+    ag2,
+    xs,
+    slots,
+    to_owner,
+    at_owner,
+    qs,
+    kvs,
+    ho,
+    to_home,
+    at_home,
+    back,
+    part1,
+    peer1,
+    out1,
+    in1,
+    part2,
+    peer2,
+    out2,
+    in2,
+    load_sem,
+    ag1_s,
+    ag1_r,
+    ag2_s,
+    ag2_r,
+    a1_s,
+    a1_r,
+    a2_s,
+    a2_r,
+    rs1_s,
+    rs1_r,
+    rs2_s,
+    rs2_r,
+):
+    devices = pool * tensor
+    rows, width = hidden_ref.shape
+    requests = devices * rows
+    head_dim = query_gain_ref.shape[1]
+    query_cols = qw.shape[1]
+    key_cols = kw.shape[1]
+    heads_here = query_cols // head_dim
+    head_count = devices * heads_here
+    kv_count = devices * key_cols // head_dim
+    per_kv = devices // kv_count
+    group = head_count // kv_count
+    hidden_units = gw.shape[1]
+    p = lax.axis_index("pool")
+    t = lax.axis_index("tensor")
+    me = p * tensor + t
+    partner = {"pool": 1 - p, "tensor": t}
+
+    loads = [
+        pltpu.make_async_copy(a, b, load_sem.at[i])
+        for i, (a, b) in enumerate(
+            [
+                (qw_hbm, qw),
+                (kw_hbm, kw),
+                (vw_hbm, vw),
+                (kc_hbm, kc),
+                (vc_hbm, vc),
+                (ow_hbm, ow),
+                (gw_hbm, gw),
+                (uw_hbm, uw),
+                (dw_hbm, dw),
+            ]
+        )
+    ]
+    for load in loads:
+        load.start()
+
+    def place(index):
+        return {"pool": lax.div(index, tensor), "tensor": lax.rem(index, tensor)}
+
+    def each(first, last, body):
+        def run(j, carry):
+            body(j)
+            return carry
+
+        lax.fori_loop(first, last, run, 0)
+
+    barrier = pltpu.get_barrier_semaphore()
+    each(
+        1,
+        devices,
+        lambda j: pl.semaphore_signal(
+            barrier, inc=1, device_id=place(lax.rem(me + j, devices)), device_id_type=MESH
+        ),
+    )
+
+    def remote(source, target, sent, received, where):
+        return pltpu.make_async_remote_copy(
+            src_ref=source,
+            dst_ref=target,
+            send_sem=sent,
+            recv_sem=received,
+            device_id=where,
+            device_id_type=MESH,
+        )
+
+    def gather(buffer, sent, received):
+        def peer_copy(j):
+            return remote(
+                buffer.at[me],
+                buffer.at[me],
+                sent.at[j],
+                received.at[me],
+                {"pool": p, "tensor": lax.rem(t + j, tensor)},
+            )
+
+        own_copy = remote(buffer.at[me], buffer.at[me], sent.at[0], received.at[me], partner)
+
+        def passed(j):
+            index = p * tensor + lax.rem(t + j, tensor)
+            return remote(
+                buffer.at[index],
+                buffer.at[index],
+                sent.at[tensor + j],
+                received.at[index],
+                partner,
+            )
+
+        def from_partner(j):
+            index = (1 - p) * tensor + lax.rem(t + j, tensor)
+            return remote(
+                buffer.at[index], buffer.at[index], sent.at[0], received.at[index], partner
+            )
+
+        each(1, tensor, lambda j: peer_copy(j).start())
+        own_copy.start()
+
+        def forward(j):
+            passed(j).wait_recv()
+            passed(j).start()
+
+        each(1, tensor, forward)
+        each(0, tensor, lambda j: from_partner(j).wait_recv())
+
+        def finish():
+            own_copy.wait_send()
+            each(1, tensor, lambda j: peer_copy(j).wait_send())
+            each(1, tensor, lambda j: passed(j).wait_send())
+
+        return finish
+
+    def exchange(outgoing, incoming, sent, received):
+        def copy(j):
+            peer = lax.rem(me + j, devices)
+            return remote(
+                outgoing.at[peer], incoming.at[me], sent.at[j], received.at[me], place(peer)
+            )
+
+        def arrival(j):
+            peer = lax.rem(me + j, devices)
+            return remote(
+                outgoing.at[peer], incoming.at[peer], sent.at[j], received.at[peer], place(peer)
+            )
+
+        each(1, devices, lambda j: copy(j).start())
+        incoming[me] = outgoing[me]
+        each(1, devices, lambda j: arrival(j).wait_recv())
+        return lambda: each(1, devices, lambda j: copy(j).wait_send())
+
+    def scatter_sum(part, peer, outgoing, incoming, sent, received):
+        swap = remote(part.at[1 - p], peer, sent.at[0], received.at[tensor], partner)
+        swap.start()
+        swap.wait_recv()
+        peer[...] = peer[...] + part[p]
+        for index in range(tensor):
+            outgoing[index] = peer[index * rows : (index + 1) * rows, :].astype(BF16)
+
+        def copy(j):
+            other = lax.rem(t + j, tensor)
+            return remote(
+                outgoing.at[other],
+                incoming.at[t],
+                sent.at[j],
+                received.at[t],
+                {"pool": p, "tensor": other},
+            )
+
+        def arrival(j):
+            other = lax.rem(t + j, tensor)
+            return remote(
+                outgoing.at[other],
+                incoming.at[other],
+                sent.at[j],
+                received.at[other],
+                {"pool": p, "tensor": other},
+            )
+
+        each(1, tensor, lambda j: copy(j).start())
+        incoming[t] = outgoing[t]
+        each(1, tensor, lambda j: arrival(j).wait_recv())
+        total = incoming[0].astype(F32)
+        for index in range(1, tensor):
+            total = total + incoming[index].astype(F32)
+
+        def finish():
+            swap.wait_send()
+            each(1, tensor, lambda j: copy(j).wait_send())
+
+        return total, finish
+
+    def spread(buffer):
+        for index in range(devices):
+            xs[index * rows : (index + 1) * rows, :] = buffer[index].astype(F32)
+
+    hidden = hidden_ref[...].astype(F32)
+    ag1[me] = rms_scale(hidden, input_gain_ref[...]).astype(BF16)
+
+    slot_row = slot_ref[...]
+    length_row = length_ref[...]
+    wide = devices * SLOTS
+    scatter_hot = (
+        lax.broadcasted_iota(jnp.int32, (wide, requests), 0) == slot_row
+    ).astype(F32).astype(BF16)
+    eye = lax.broadcasted_iota(jnp.int32, (requests, requests), 0) == lax.broadcasted_iota(
+        jnp.int32, (requests, requests), 1
+    )
+    slot_col = jnp.sum(
+        jnp.where(eye, jnp.broadcast_to(slot_row, (requests, requests)), 0).astype(F32),
+        axis=1,
+        keepdims=True,
+    ).astype(jnp.int32)
+    gather_hot = (
+        lax.broadcasted_iota(jnp.int32, (requests, wide), 1) == slot_col
+    ).astype(F32).astype(BF16)
+    span = 2 * SLOTS
+    place_id = lax.rem(lax.broadcasted_iota(jnp.int32, (span, requests), 0), SLOTS)
+    slot_wide = jnp.broadcast_to(slot_row, (span, requests))
+    length_wide = jnp.broadcast_to(length_row, (span, requests)).astype(F32)
+    base = me * SLOTS
+    slot_length = jnp.sum(
+        jnp.where(slot_wide == base + place_id, length_wide, 0.0), axis=1, keepdims=True
+    )
+    slot_offset = jnp.sum(
+        jnp.where((slot_wide >= base) & (slot_wide < base + place_id), length_wide, 0.0),
+        axis=1,
+        keepdims=True,
+    )
+    angles = slot_length * frequency_ref[...]
+    cosine = jnp.cos(angles)
+    lane = lax.broadcasted_iota(jnp.int32, (span, head_dim), 1)
+    sine_part = jnp.where(lane < head_dim // 2, -jnp.sin(angles), jnp.sin(angles))
+    pool_tokens = kc.shape[0]
+    token = lax.broadcasted_iota(jnp.int32, (span, pool_tokens), 1).astype(F32)
+    inside = jnp.where(
+        (token >= slot_offset) & (token < slot_offset + slot_length), 1.0, 0.0
+    )
+
+    def turn(values, scale, copies):
+        scaled = rms_scale(values, scale)
+        return scaled * jnp.tile(cosine, (copies, 1)) + pltpu.roll(
+            scaled, head_dim // 2, 1
+        ) * jnp.tile(sine_part, (copies, 1))
+
+    pl.semaphore_wait(barrier, devices - 1)
+    done = [gather(ag1, ag1_s, ag1_r)]
+    spread(ag1)
+    for load in loads[:3]:
+        load.wait()
+    chunk = math.gcd(width, 512)
+
+    def project(i, carry):
+        at = pl.ds(pl.multiple_of(i * chunk, chunk), chunk)
+        left = xs[:, at].astype(BF16)
+        return tuple(
+            acc + jnp.dot(left, w[at, :], preferred_element_type=F32)
+            for acc, w in zip(carry, (qw, kw, vw))
+        )
+
+    query_part, key_part, value_part = lax.fori_loop(
+        0,
+        width // chunk,
+        project,
+        (
+            jnp.zeros((requests, query_cols), F32),
+            jnp.zeros((requests, key_cols), F32),
+            jnp.zeros((requests, key_cols), F32),
+        ),
+    )
+
+    def shift(count, amount):
+        low = lax.broadcasted_iota(jnp.int32, (count, head_dim), 0)
+        high = lax.broadcasted_iota(jnp.int32, (count, head_dim), 1)
+        return (low + amount == high).astype(F32).astype(BF16)
+
+    kv_part = jnp.dot(
+        key_part.astype(BF16), shift(key_cols, 0), preferred_element_type=F32
+    ) + jnp.dot(value_part.astype(BF16), shift(key_cols, key_cols), preferred_element_type=F32)
+    slots[:, :query_cols] = jnp.dot(
+        scatter_hot, query_part.astype(BF16), preferred_element_type=F32
+    )
+    slots[:, query_cols:] = jnp.dot(
+        scatter_hot, kv_part.astype(BF16), preferred_element_type=F32
+    )
+    for index in range(devices):
+        to_owner[index] = slots[index * SLOTS : (index + 1) * SLOTS, :].astype(BF16)
+    done.append(exchange(to_owner, at_owner, a1_s, a1_r))
+
+    for index in range(devices):
+        arrived = at_owner[index].astype(F32)
+        for j in range(heads_here):
+            at = (index * heads_here + j) * SLOTS
+            qs[at : at + SLOTS, :] = arrived[:, j * head_dim : (j + 1) * head_dim]
+        at = (index // per_kv) * span
+        lanes = (index % per_kv) * head_dim
+        kvs[at : at + SLOTS, lanes : lanes + head_dim] = arrived[:, query_cols:]
+        kvs[at + SLOTS : at + span, lanes : lanes + head_dim] = arrived[:, query_cols:]
+
+    low = lax.broadcasted_iota(jnp.int32, (per_kv * head_dim, head_dim), 0)
+    high = lax.broadcasted_iota(jnp.int32, (per_kv * head_dim, head_dim), 1)
+    piece = lax.div(low, head_dim)
+    inner = lax.rem(low, head_dim)
+    key_hot = ((inner < key_cols) & (piece * key_cols + inner == high)).astype(F32).astype(BF16)
+    value_hot = (
+        ((inner >= key_cols) & (inner < 2 * key_cols) & (piece * key_cols + inner - key_cols == high))
+        .astype(F32)
+        .astype(BF16)
+    )
+    pieces = kvs[...].astype(BF16)
+    key_new = turn(
+        jnp.dot(pieces, key_hot, preferred_element_type=F32), key_gain_ref[...], kv_count
+    ).astype(BF16)
+    value_new = jnp.dot(pieces, value_hot, preferred_element_type=F32)
+    scale_factor = 1.0 / math.sqrt(head_dim)
+    block = group * SLOTS
+    copies = block // span
+    allowed = jnp.tile(inside, (copies, 1)) > 0.5
+    for load in loads[3:5]:
+        load.wait()
+    for k in range(kv_count):
+        query = turn(qs[k * block : (k + 1) * block, :], query_gain_ref[...], copies).astype(BF16)
+        lanes = slice(k * head_dim, (k + 1) * head_dim)
+        scores = (
+            lax.dot_general(
+                query, kc[:, lanes], (((1,), (1,)), ((), ())), preferred_element_type=F32
+            )
+            * scale_factor
+        )
+        own_key = jnp.tile(key_new[k * span : (k + 1) * span, :].astype(F32), (copies, 1))
+        own_value = jnp.tile(value_new[k * span : (k + 1) * span, :], (copies, 1))
+        own_score = jnp.sum(query.astype(F32) * own_key, axis=1, keepdims=True) * scale_factor
+        scores = jnp.where(allowed, scores, -1e30)
+        largest = jnp.maximum(jnp.max(scores, axis=1, keepdims=True), own_score)
+        weights = jnp.exp(scores - largest)
+        own_weight = jnp.exp(own_score - largest)
+        denominator = jnp.sum(weights, axis=1, keepdims=True) + own_weight
+        summed = jnp.dot(weights.astype(BF16), vc[:, lanes], preferred_element_type=F32)
+        summed = summed + own_weight.astype(BF16).astype(F32) * own_value
+        ho[k * block : (k + 1) * block, :] = summed / denominator
+    for index in range(devices):
+        for j in range(heads_here):
+            at = (index * heads_here + j) * SLOTS
+            to_home[index, :, j * head_dim : (j + 1) * head_dim] = ho[at : at + SLOTS, :].astype(BF16)
+    done.append(exchange(to_home, at_home, a2_s, a2_r))
+    for index in range(devices):
+        back[index * SLOTS : (index + 1) * SLOTS, :] = at_home[index].astype(F32)
+    head_rows = jnp.dot(
+        gather_hot, back[...].astype(BF16), preferred_element_type=F32
+    ).astype(BF16)
+
+    half = tensor * rows
+
+    def multiply(left, weight, part):
+        def columns(i):
+            at = pl.ds(pl.multiple_of(i * chunk, chunk), chunk)
+            product = jnp.dot(left, weight[:, at], preferred_element_type=F32)
+            for q in range(pool):
+                part[q, :, at] = product[q * half : (q + 1) * half, :]
+
+        each(0, width // chunk, columns)
+
+    loads[5].wait()
+    multiply(head_rows, ow, part1)
+    total, finish = scatter_sum(part1, peer1, out1, in1, rs1_s, rs1_r)
+    done.append(finish)
+    mixed = (total + hidden).astype(BF16)
+    mixed_ref[...] = mixed
+    ag2[me] = rms_scale(mixed, post_gain_ref[...]).astype(BF16)
+    done.append(gather(ag2, ag2_s, ag2_r))
+    spread(ag2)
+    loads[6].wait()
+    loads[7].wait()
+
+    def expand(i, carry):
+        at = pl.ds(pl.multiple_of(i * chunk, chunk), chunk)
+        left = xs[:, at].astype(BF16)
+        return tuple(
+            acc + jnp.dot(left, w[at, :], preferred_element_type=F32)
+            for acc, w in zip(carry, (gw, uw))
+        )
+
+    gate_part, up_part = lax.fori_loop(
+        0,
+        width // chunk,
+        expand,
+        (jnp.zeros((requests, hidden_units), F32), jnp.zeros((requests, hidden_units), F32)),
+    )
+    activated = (gate_part / (1.0 + jnp.exp(-gate_part)) * up_part).astype(BF16)
+    loads[8].wait()
+    multiply(activated, dw, part2)
+    total, finish = scatter_sum(part2, peer2, out2, in2, rs2_s, rs2_r)
+    done.append(finish)
+    final_ref[...] = (mixed_ref[...].astype(F32) + total).astype(BF16)
+    for finish in done:
+        finish()
+
+
+def fused(pool, tensor, *operands):
+    (
+        hidden,
+        input_gain,
+        query_weight,
+        key_weight,
+        value_weight,
+        query_gain,
+        key_gain,
+        output_weight,
+        post_gain,
+        gate_weight,
+        up_weight,
+        down_weight,
+        key_cache,
+        value_cache,
+        lengths,
+        request_slot,
+    ) = operands
+    devices = pool * tensor
+    rows, width = hidden.shape
+    head_dim = query_gain.shape[0]
+    query_cols = query_weight.shape[1]
+    key_cols = key_weight.shape[1]
+    heads_here = query_cols // head_dim
+    kv_count = devices * key_cols // head_dim
+    per_kv = devices // kv_count
+    requests = devices * rows
+    half_width = head_dim // 2
+    frequency = theta ** (-jnp.arange(half_width, dtype=jnp.float32) * 2.0 / head_dim)
+    frequency = jnp.concatenate([frequency, frequency])[None, :]
+    heavy = (
+        query_weight,
+        key_weight,
+        value_weight,
+        output_weight,
+        gate_weight,
+        up_weight,
+        down_weight,
+        key_cache,
+        value_cache,
+    )
+    dma = pltpu.SemaphoreType.DMA
+    sent_cols = query_cols + head_dim
+    sums = [
+        pltpu.VMEM((pool, tensor * rows, width), F32),
+        pltpu.VMEM((tensor * rows, width), F32),
+        pltpu.VMEM((tensor, rows, width), BF16),
+        pltpu.VMEM((tensor, rows, width), BF16),
+    ]
+    scratch = (
+        [pltpu.VMEM(w.shape, w.dtype) for w in heavy]
+        + [pltpu.VMEM((devices, rows, width), BF16)] * 2
+        + [
+            pltpu.VMEM((requests, width), F32),
+            pltpu.VMEM((devices * SLOTS, sent_cols), F32),
+            pltpu.VMEM((devices, SLOTS, sent_cols), BF16),
+            pltpu.VMEM((devices, SLOTS, sent_cols), BF16),
+            pltpu.VMEM((devices * heads_here * SLOTS, head_dim), F32),
+            pltpu.VMEM((kv_count * 2 * SLOTS, per_kv * head_dim), F32),
+            pltpu.VMEM((devices * heads_here * SLOTS, head_dim), F32),
+            pltpu.VMEM((devices, SLOTS, query_cols), BF16),
+            pltpu.VMEM((devices, SLOTS, query_cols), BF16),
+            pltpu.VMEM((devices * SLOTS, query_cols), F32),
+        ]
+        + sums
+        + sums
+        + [dma((len(heavy),))]
+        + [dma((2 * tensor,)), dma((devices,))] * 2
+        + [dma((devices,)), dma((devices,))] * 2
+        + [dma((tensor,)), dma((tensor + 1,))] * 2
+    )
+    vmem = pl.BlockSpec(memory_space=pltpu.VMEM)
+    hbm = pl.BlockSpec(memory_space=pl.ANY)
+    row = jax.ShapeDtypeStruct(hidden.shape, hidden.dtype)
+    return pl.pallas_call(
+        functools.partial(step_kernel, pool, tensor),
+        out_shape=(row, row),
+        in_specs=[vmem] * 8 + [hbm] * len(heavy),
+        out_specs=(vmem, vmem),
+        scratch_shapes=scratch,
+        compiler_params=pltpu.CompilerParams(
+            collective_id=0, has_side_effects=True, vmem_limit_bytes=62 * 1024 * 1024
+        ),
+    )(
+        hidden,
+        input_gain[None, :],
+        query_gain[None, :],
+        key_gain[None, :],
+        post_gain[None, :],
+        lengths[None, :],
+        request_slot[None, :],
+        frequency,
+        *heavy,
+    )
+
+
+def dispatch(pool, tensor, *operands):
+    query_cols = operands[2].shape[1]
+    key_cols = operands[3].shape[1]
+    head_dim = operands[5].shape[0]
+    whole_heads = query_cols % head_dim == 0 and head_dim % key_cols == 0
+    if pool == 2 and whole_heads and 2 * key_cols <= head_dim:
+        return fused(pool, tensor, *operands)
+    return on_device(*operands)
+
+
 def solution(mesh):
     placed = (
         P(("groups", "pool", "tensor"), None),
@@ -170,7 +725,7 @@
         P("groups"),
     )
     return jax.shard_map(
-        on_device,
+        functools.partial(dispatch, mesh.shape["pool"], mesh.shape["tensor"]),
         mesh=mesh,
         in_specs=placed,
         out_specs=(P(("groups", "pool", "tensor"), None), P(("groups", "pool", "tensor"), None)),

time: 271 us -> 91.7 us (0.34)
  blocking collectives: 102 us -> 0 us
  waiting for transfers between devices: 97.3 us -> 0 us
  Pallas kernels: 0 us -> 57.1 us
  matrix products: 26.6 us -> 0 us
  local copies, waits for them, and re-layouts: 11 us -> 32.5 us
  between operations: 15 us -> 0.64 us
  starting transfers between devices: 9.46 us -> 0 us
  other arithmetic: 8.24 us -> 0.6 us
    unnamed x2 -> x0, waiting for transfers between devices: 90.8 us -> none
    psum x1 -> x0, blocking collectives: 66.3 us -> none  [on_device(): totals = lax.psum(partial_value, ('pool', 'tensor'))]
    pallas_call x0 -> x1, Pallas kernels: none -> 57.1 us  [fused(): pl.pallas_call(functools.partial(step_kernel, pool, tensor), out_shape=(r...]
    all_gather x1 -> x0, blocking collectives: 36.2 us -> none  [on_device(): shard_rows = lax.all_gather(normed, ('pool', 'tensor'), axis=0, tiled=True)]
    unnamed x22 -> x6, local copies, waits for them, and re-layouts: 0.93 us -> 32.5 us
    dot_general x9 -> x0, matrix products: 26.6 us -> none  [the longest x1 11.4 us: on_device(): jnp.dot(activated, down_weight, preferred_element_type=jnp.float32)]
    all_to_all x2 -> x0, starting transfers between devices: 9.42 us -> none  [the longest x1 5.92 us: on_device(): lax.all_to_all(head_out, ('pool', 'tensor'), split_axis=1, concat_axis=0,...]
    reshape x6 -> x0, local copies, waits for them, and re-layouts: 9.28 us -> none  [the longest x1 3.99 us: on_device(): cached_values = value_cache.reshape(pool_tokens, kv_count, head_dim)]
  transfers between devices with their start and end apart: 3 -> 0, of which waited for: 2 -> 0; matrix products, arithmetic and copies ran while one was open for 3% -> 0% of each run, Pallas kernels for 0% -> 0%
where the time goes in v1:
time: 91.7 us; the launch traced here: 90.8 us
  Pallas kernels  57.1 us (62%)
  local copies, waits for them, and re-layouts  32.5 us (35%)
    pallas_call x1, Pallas kernels, fused(): pl.pallas_call(functools.partial(step_kernel, pool, tensor), out_shape=(r...  57.1 us
    unnamed x6, local copies, waits for them, and re-layouts  32.5 us

profile of v1, /device:TPU:0, one launch (start us, length us, event | category | flops | bytes accessed | tf_op | source)
XLA Modules:
  0.0 90.8 jit_solution(13529628687337288391)
XLA Ops:
  0.6 0.6 maximum_bitcast_fusion.frequency_ref
  1.2 2.3 %copy.18.kw_hbm = bf16[5120,32]{1,0:T(8,128)(2,1)} copy(bf16[5120,32]{0,1:T(8,128)(2,1)} %param.19) | data formatting | bytes 655360 | tf_op args[3]
  3.5 2.3 %copy.19.vw_hbm = bf16[5120,32]{1,0:T(8,128)(2,1)} copy(bf16[5120,32]{0,1:T(8,128)(2,1)} %param.20) | data formatting | bytes 655360 | tf_op args[4]
  5.8 12.6 %copy.20.gw_hbm = bf16[5120,800]{1,0:T(8,128)(2,1)} copy(bf16[5120,800]{0,1:T(8,128)(2,1)} %param.25) | data formatting | bytes 16384000 | tf_op args[9]
  18.4 12.6 %copy.21.uw_hbm = bf16[5120,800]{1,0:T(8,128)(2,1)} copy(bf16[5120,800]{0,1:T(8,128)(2,1)} %param.26) | data formatting | bytes 16384000 | tf_op args[10]
  31.0 57.1 %shard_map.167 = (bf16[2,5120]{1,0:T(2,128)(2,1)}, bf16[2,5120]{1,0:T(2,128)(2,1)}) custom-call(bf16[2,5120]{1,0:T(2,128)(2,1)} %hidden_ref.1, f32[1,5120]{1,0:T(1,128)} %bitcast.8, f32[1,128]{1,0:T(1,128)} %bitcast.10, f32[1,128]{1,0:T(1,128)} %bitcast.11, f32[1,5120]{1,0:T(1,128)} %bitcast.9, s32[1,32]{1,0:T(1,128)} %bitcast.12, s32[1,32]{1,0:T(1,128)} %bitcast.13, ...), custom_call_target="tpu_custom_call" | custom-call | tf_op jit(solution)/shard_map/pallas_call | solution.py:676
  88.1 1.3 %copy.24 = bf16[2,5120]{1,0:T(2,128)(2,1)} copy(bf16[2,5120]{1,0:T(2,128)(2,1)} %get-tuple-element.4) | data formatting | bytes 40960
  89.5 1.3 %copy.25 = bf16[2,5120]{1,0:T(2,128)(2,1)} copy(bf16[2,5120]{1,0:T(2,128)(2,1)} %get-tuple-element.5) | data formatting | bytes 40960
  (1 shorter events, 0.0 us)

commit v2 on v1

--- a/solution.py
+++ b/solution.py
@@ -3,6 +3,7 @@
 
 import jax
 import jax.numpy as jnp
+import numpy as np
 from jax import lax
 from jax.experimental import pallas as pl
 from jax.experimental.pallas import tpu as pltpu
@@ -228,13 +229,13 @@
     requests = devices * rows
     head_dim = query_gain_ref.shape[1]
     query_cols = qw.shape[1]
-    key_cols = kw.shape[1]
+    key_cols = kw.shape[0]
     heads_here = query_cols // head_dim
     head_count = devices * heads_here
     kv_count = devices * key_cols // head_dim
     per_kv = devices // kv_count
     group = head_count // kv_count
-    hidden_units = gw.shape[1]
+    hidden_units = gw.shape[0]
     p = lax.axis_index("pool")
     t = lax.axis_index("tensor")
     me = p * tensor + t
@@ -452,12 +453,24 @@
         load.wait()
     chunk = math.gcd(width, 512)
 
+    def turned(left, weight, at):
+        return lax.dot_general(
+            left, weight[:, at], (((1,), (1,)), ((), ())), preferred_element_type=F32
+        )
+
     def project(i, carry):
         at = pl.ds(pl.multiple_of(i * chunk, chunk), chunk)
         left = xs[:, at].astype(BF16)
         return tuple(
-            acc + jnp.dot(left, w[at, :], preferred_element_type=F32)
-            for acc, w in zip(carry, (qw, kw, vw))
+            acc + product
+            for acc, product in zip(
+                carry,
+                (
+                    jnp.dot(left, qw[at, :], preferred_element_type=F32),
+                    turned(left, kw, at),
+                    turned(left, vw, at),
+                ),
+            )
         )
 
     query_part, key_part, value_part = lax.fori_loop(
@@ -578,7 +591,7 @@
         at = pl.ds(pl.multiple_of(i * chunk, chunk), chunk)
         left = xs[:, at].astype(BF16)
         return tuple(
-            acc + jnp.dot(left, w[at, :], preferred_element_type=F32)
+            acc + turned(left, w, at)
             for acc, w in zip(carry, (gw, uw))
         )
 
@@ -627,15 +640,15 @@
     per_kv = devices // kv_count
     requests = devices * rows
     half_width = head_dim // 2
-    frequency = theta ** (-jnp.arange(half_width, dtype=jnp.float32) * 2.0 / head_dim)
-    frequency = jnp.concatenate([frequency, frequency])[None, :]
+    frequency = theta ** (-np.arange(half_width) * 2.0 / head_dim)
+    frequency = np.concatenate([frequency, frequency])[None, :].astype(np.float32)
     heavy = (
         query_weight,
-        key_weight,
-        value_weight,
+        key_weight.T,
+        value_weight.T,
         output_weight,
-        gate_weight,
-        up_weight,
+        gate_weight.T,
+        up_weight.T,
         down_weight,
         key_cache,
         value_cache,

time: 91.7 us -> 62.4 us (0.68)
  local copies, waits for them, and re-layouts: 32.5 us -> 2.7 us
  Pallas kernels: 57.1 us -> 58.7 us
    unnamed x6 -> x2, local copies, waits for them, and re-layouts: 32.5 us -> 2.7 us
    pallas_call x1, Pallas kernels: 57.1 us -> 58.7 us  [fused(): pl.pallas_call(functools.partial(step_kernel, pool, tensor), out_shape=(r...]
where the time goes in v2:
time: 62.4 us; the launch traced here: 62.1 us
  Pallas kernels  58.7 us (94%)
  local copies, waits for them, and re-layouts  2.7 us (4%)
  between operations  0.65 us (1%)
    pallas_call x1, Pallas kernels, fused(): pl.pallas_call(functools.partial(step_kernel, pool, tensor), out_shape=(r...  58.7 us
    unnamed x2, local copies, waits for them, and re-layouts  2.7 us

profile of v2, /device:TPU:0, one launch (start us, length us, event | category | flops | bytes accessed | tf_op | source)
XLA Modules:
  0.0 62.1 jit_solution(15729702048489439781)
XLA Ops:
  0.6 58.7 %shard_map.176 = (bf16[2,5120]{1,0:T(2,128)(2,1)}, bf16[2,5120]{1,0:T(2,128)(2,1)}) custom-call(bf16[2,5120]{1,0:T(2,128)(2,1)} %hidden_ref.1, f32[1,5120]{1,0:T(1,128)} %bitcast.14, f32[1,128]{1,0:T(1,128)} %bitcast.16, f32[1,128]{1,0:T(1,128)} %bitcast.17, f32[1,5120]{1,0:T(1,128)} %bitcast.15, s32[1,32]{1,0:T(1,128)} %bitcast.18, s32[1,32]{1,0:T(1,128)} %bitcast.19, ...), custom_call_target="tpu_custom_call" | custom-call | tf_op jit(solution)/shard_map/pallas_call | solution.py:689
  59.4 1.3 %copy.21 = bf16[2,5120]{1,0:T(2,128)(2,1)} copy(bf16[2,5120]{1,0:T(2,128)(2,1)} %get-tuple-element.4) | data formatting | bytes 40960
  60.7 1.3 %copy.22 = bf16[2,5120]{1,0:T(2,128)(2,1)} copy(bf16[2,5120]{1,0:T(2,128)(2,1)} %get-tuple-element.5) | data formatting | bytes 40960

commit v3 on v2

--- a/solution.py
+++ b/solution.py
@@ -156,6 +156,7 @@
 
 MESH = pl.DeviceIdType.MESH
 F32 = jnp.float32
+SPLIT = 2
 BF16 = jnp.bfloat16
 
 
@@ -179,8 +180,7 @@
     dw_hbm,
     kc_hbm,
     vc_hbm,
-    mixed_ref,
-    final_ref,
+    both_ref,
     qw,
     kw,
     vw,
@@ -289,50 +289,72 @@
             device_id_type=MESH,
         )
 
-    def gather(buffer, sent, received):
-        def peer_copy(j):
-            return remote(
-                buffer.at[me],
-                buffer.at[me],
-                sent.at[j],
-                received.at[me],
+    def gather(buffer, sent, received, lead, advance, carry):
+        split = buffer.shape[0]
+
+        def peer_copy(c, j):
+            return remote(
+                buffer.at[c, me],
+                buffer.at[c, me],
+                sent.at[c, j],
+                received.at[c, me],
                 {"pool": p, "tensor": lax.rem(t + j, tensor)},
             )
 
-        own_copy = remote(buffer.at[me], buffer.at[me], sent.at[0], received.at[me], partner)
-
-        def passed(j):
+        def own_copy(c):
+            return remote(
+                buffer.at[c, me], buffer.at[c, me], sent.at[c, 0], received.at[c, me], partner
+            )
+
+        def passed(c, j):
             index = p * tensor + lax.rem(t + j, tensor)
             return remote(
-                buffer.at[index],
-                buffer.at[index],
-                sent.at[tensor + j],
-                received.at[index],
+                buffer.at[c, index],
+                buffer.at[c, index],
+                sent.at[c, tensor + j],
+                received.at[c, index],
                 partner,
             )
 
-        def from_partner(j):
+        def from_partner(c, j):
             index = (1 - p) * tensor + lax.rem(t + j, tensor)
             return remote(
-                buffer.at[index], buffer.at[index], sent.at[0], received.at[index], partner
-            )
-
-        each(1, tensor, lambda j: peer_copy(j).start())
-        own_copy.start()
-
-        def forward(j):
-            passed(j).wait_recv()
-            passed(j).start()
-
-        each(1, tensor, forward)
-        each(0, tensor, lambda j: from_partner(j).wait_recv())
+                buffer.at[c, index],
+                buffer.at[c, index],
+                sent.at[c, 0],
+                received.at[c, index],
+                partner,
+            )
+
+        def forward(c, j):
+            passed(c, j).wait_recv()
+            passed(c, j).start()
+
+        for c in range(split):
+            each(1, tensor, lambda j: peer_copy(c, j).start())
+            own_copy(c).start()
+        each(1, tensor, lambda j: forward(0, j))
+        steps = width // split // chunk
+        for c in range(split):
+            each(0, tensor, lambda j: from_partner(c, j).wait_recv())
+            for index in range(devices):
+                xs[index * rows : (index + 1) * rows, c * width // split : (c + 1) * width // split] = (
+                    buffer[c, index].astype(F32)
+                )
+            first = c * steps
+            if c + 1 < split:
+                carry = lax.fori_loop(first, first + lead, advance, carry)
+                each(1, tensor, lambda j: forward(c + 1, j))
+                first = first + lead
+            carry = lax.fori_loop(first, (c + 1) * steps, advance, carry)
 
         def finish():
-            own_copy.wait_send()
-            each(1, tensor, lambda j: peer_copy(j).wait_send())
-            each(1, tensor, lambda j: passed(j).wait_send())
-
-        return finish
+            for c in range(split):
+                own_copy(c).wait_send()
+                each(1, tensor, lambda j: peer_copy(c, j).wait_send())
+                each(1, tensor, lambda j: passed(c, j).wait_send())
+
+        return carry, finish
 
     def exchange(outgoing, incoming, sent, received):
         def copy(j):
@@ -352,53 +374,80 @@
         each(1, devices, lambda j: arrival(j).wait_recv())
         return lambda: each(1, devices, lambda j: copy(j).wait_send())
 
-    def scatter_sum(part, peer, outgoing, incoming, sent, received):
-        swap = remote(part.at[1 - p], peer, sent.at[0], received.at[tensor], partner)
-        swap.start()
-        swap.wait_recv()
-        peer[...] = peer[...] + part[p]
-        for index in range(tensor):
-            outgoing[index] = peer[index * rows : (index + 1) * rows, :].astype(BF16)
-
-        def copy(j):
+    def scatter_sum(left, weight, part, peer, outgoing, incoming, sent, received):
+        split = part.shape[0]
+        wide = width // split
+
+        def swap(c):
+            return remote(
+                part.at[c, 1 - p], peer.at[c], sent.at[c, 0], received.at[c, tensor], partner
+            )
+
+        def copy(c, j):
             other = lax.rem(t + j, tensor)
             return remote(
-                outgoing.at[other],
-                incoming.at[t],
-                sent.at[j],
-                received.at[t],
+                outgoing.at[c, other],
+                incoming.at[c, t],
+                sent.at[c, j],
+                received.at[c, t],
                 {"pool": p, "tensor": other},
             )
 
-        def arrival(j):
+        def arrival(c, j):
             other = lax.rem(t + j, tensor)
             return remote(
-                outgoing.at[other],
-                incoming.at[other],
-                sent.at[j],
-                received.at[other],
+                outgoing.at[c, other],
+                incoming.at[c, other],
+                sent.at[c, j],
+                received.at[c, other],
                 {"pool": p, "tensor": other},
             )
 
-        each(1, tensor, lambda j: copy(j).start())
-        incoming[t] = outgoing[t]
-        each(1, tensor, lambda j: arrival(j).wait_recv())
-        total = incoming[0].astype(F32)
-        for index in range(1, tensor):
-            total = total + incoming[index].astype(F32)
+        for c in range(split):
+
+            def columns(i):
+                near = pl.multiple_of(i * chunk, chunk)
+                product = jnp.dot(
+                    left, weight[:, pl.ds(c * wide + near, chunk)], preferred_element_type=F32
+                )
+                for q in range(pool):
+                    part[c, q, :, pl.ds(near, chunk)] = product[q * half : (q + 1) * half, :]
+
+            each(0, wide // chunk, columns)
+            swap(c).start()
+        for c in range(split):
+            swap(c).wait_recv()
+            peer[c] = peer[c] + part[c, p]
+            for index in range(tensor):
+                outgoing[c, index] = peer[c, index * rows : (index + 1) * rows, :].astype(BF16)
+            each(1, tensor, lambda j: copy(c, j).start())
+            incoming[c, t] = outgoing[c, t]
+        totals = []
+        for c in range(split):
+            each(1, tensor, lambda j: arrival(c, j).wait_recv())
+            total = incoming[c, 0].astype(F32)
+            for index in range(1, tensor):
+                total = total + incoming[c, index].astype(F32)
+            totals.append(total)
 
         def finish():
-            swap.wait_send()
-            each(1, tensor, lambda j: copy(j).wait_send())
-
-        return total, finish
-
-    def spread(buffer):
-        for index in range(devices):
-            xs[index * rows : (index + 1) * rows, :] = buffer[index].astype(F32)
+            for c in range(split):
+                swap(c).wait_send()
+                each(1, tensor, lambda j: copy(c, j).wait_send())
+
+        return jnp.concatenate(totals, axis=1), finish
+
+    split = ag1.shape[0]
+    chunk = math.gcd(width // split, 512)
+    half = tensor * rows
+
+    def offer(buffer, values):
+        wide = width // split
+        for c in range(split):
+            buffer[c, me] = values[:, c * wide : (c + 1) * wide].astype(BF16)
 
     hidden = hidden_ref[...].astype(F32)
-    ag1[me] = rms_scale(hidden, input_gain_ref[...]).astype(BF16)
+    offer(ag1, rms_scale(hidden, input_gain_ref[...]))
 
     slot_row = slot_ref[...]
     length_row = length_ref[...]
@@ -447,11 +496,8 @@
         ) * jnp.tile(sine_part, (copies, 1))
 
     pl.semaphore_wait(barrier, devices - 1)
-    done = [gather(ag1, ag1_s, ag1_r)]
-    spread(ag1)
     for load in loads[:3]:
         load.wait()
-    chunk = math.gcd(width, 512)
 
     def turned(left, weight, at):
         return lax.dot_general(
@@ -473,9 +519,11 @@
             )
         )
 
-    query_part, key_part, value_part = lax.fori_loop(
-        0,
-        width // chunk,
+    (query_part, key_part, value_part), finish = gather(
+        ag1,
+        ag1_s,
+        ag1_r,
+        1,
         project,
         (
             jnp.zeros((requests, query_cols), F32),
@@ -483,6 +531,8 @@
             jnp.zeros((requests, key_cols), F32),
         ),
     )
+
+    done = [finish]
 
     def shift(count, amount):
         low = lax.broadcasted_iota(jnp.int32, (count, head_dim), 0)
@@ -564,26 +614,12 @@
         gather_hot, back[...].astype(BF16), preferred_element_type=F32
     ).astype(BF16)
 
-    half = tensor * rows
-
-    def multiply(left, weight, part):
-        def columns(i):
-            at = pl.ds(pl.multiple_of(i * chunk, chunk), chunk)
-            product = jnp.dot(left, weight[:, at], preferred_element_type=F32)
-            for q in range(pool):
-                part[q, :, at] = product[q * half : (q + 1) * half, :]
-
-        each(0, width // chunk, columns)
-
     loads[5].wait()
-    multiply(head_rows, ow, part1)
-    total, finish = scatter_sum(part1, peer1, out1, in1, rs1_s, rs1_r)
+    total, finish = scatter_sum(head_rows, ow, part1, peer1, out1, in1, rs1_s, rs1_r)
     done.append(finish)
     mixed = (total + hidden).astype(BF16)
-    mixed_ref[...] = mixed
-    ag2[me] = rms_scale(mixed, post_gain_ref[...]).astype(BF16)
-    done.append(gather(ag2, ag2_s, ag2_r))
-    spread(ag2)
+    both_ref[0] = mixed.astype(F32)
+    offer(ag2, rms_scale(mixed, post_gain_ref[...]))
     loads[6].wait()
     loads[7].wait()
 
@@ -595,18 +631,20 @@
             for acc, w in zip(carry, (gw, uw))
         )
 
-    gate_part, up_part = lax.fori_loop(
-        0,
-        width // chunk,
+    (gate_part, up_part), finish = gather(
+        ag2,
+        ag2_s,
+        ag2_r,
+        2,
         expand,
         (jnp.zeros((requests, hidden_units), F32), jnp.zeros((requests, hidden_units), F32)),
     )
+    done.append(finish)
     activated = (gate_part / (1.0 + jnp.exp(-gate_part)) * up_part).astype(BF16)
     loads[8].wait()
-    multiply(activated, dw, part2)
-    total, finish = scatter_sum(part2, peer2, out2, in2, rs2_s, rs2_r)
+    total, finish = scatter_sum(activated, dw, part2, peer2, out2, in2, rs2_s, rs2_r)
     done.append(finish)
-    final_ref[...] = (mixed_ref[...].astype(F32) + total).astype(BF16)
+    both_ref[1] = both_ref[0] + total
     for finish in done:
         finish()
 
@@ -656,14 +694,14 @@
     dma = pltpu.SemaphoreType.DMA
     sent_cols = query_cols + head_dim
     sums = [
-        pltpu.VMEM((pool, tensor * rows, width), F32),
-        pltpu.VMEM((tensor * rows, width), F32),
-        pltpu.VMEM((tensor, rows, width), BF16),
-        pltpu.VMEM((tensor, rows, width), BF16),
+        pltpu.VMEM((SPLIT, pool, tensor * rows, width // SPLIT), F32),
+        pltpu.VMEM((SPLIT, tensor * rows, width // SPLIT), F32),
+        pltpu.VMEM((SPLIT, tensor, rows, width // SPLIT), BF16),
+        pltpu.VMEM((SPLIT, tensor, rows, width // SPLIT), BF16),
     ]
     scratch = (
         [pltpu.VMEM(w.shape, w.dtype) for w in heavy]
-        + [pltpu.VMEM((devices, rows, width), BF16)] * 2
+        + [pltpu.VMEM((SPLIT, devices, rows, width // SPLIT), BF16)] * 2
         + [
             pltpu.VMEM((requests, width), F32),
             pltpu.VMEM((devices * SLOTS, sent_cols), F32),
@@ -679,18 +717,18 @@
         + sums
         + sums
         + [dma((len(heavy),))]
-        + [dma((2 * tensor,)), dma((devices,))] * 2
+        + [dma((SPLIT, 2 * tensor)), dma((SPLIT, devices))] * 2
         + [dma((devices,)), dma((devices,))] * 2
-        + [dma((tensor,)), dma((tensor + 1,))] * 2
+        + [dma((SPLIT, tensor)), dma((SPLIT, tensor + 1))] * 2
     )
     vmem = pl.BlockSpec(memory_space=pltpu.VMEM)
     hbm = pl.BlockSpec(memory_space=pl.ANY)
-    row = jax.ShapeDtypeStruct(hidden.shape, hidden.dtype)
-    return pl.pallas_call(
+    both = jax.ShapeDtypeStruct((2, *hidden.shape), F32)
+    both = pl.pallas_call(
         functools.partial(step_kernel, pool, tensor),
-        out_shape=(row, row),
+        out_shape=both,
         in_specs=[vmem] * 8 + [hbm] * len(heavy),
-        out_specs=(vmem, vmem),
+        out_specs=vmem,
         scratch_shapes=scratch,
         compiler_params=pltpu.CompilerParams(
             collective_id=0, has_side_effects=True, vmem_limit_bytes=62 * 1024 * 1024
@@ -706,6 +744,7 @@
         frequency,
         *heavy,
     )
+    return both[0].astype(hidden.dtype), both[1].astype(hidden.dtype)
 
 
 def dispatch(pool, tensor, *operands):
@@ -713,7 +752,8 @@
     key_cols = operands[3].shape[1]
     head_dim = operands[5].shape[0]
     whole_heads = query_cols % head_dim == 0 and head_dim % key_cols == 0
-    if pool == 2 and whole_heads and 2 * key_cols <= head_dim:
+    lanes = operands[0].shape[1] % (SPLIT * 512) == 0
+    if pool == 2 and lanes and whole_heads and 2 * key_cols <= head_dim:
         return fused(pool, tensor, *operands)
     return on_device(*operands)
 

time: 62.4 us -> 60.8 us (0.974)
  local copies, waits for them, and re-layouts: 2.7 us -> 0.64 us
  other arithmetic: 0 us -> 0.92 us
    unnamed x2 -> x0, local copies, waits for them, and re-layouts: 2.7 us -> none
    another operation x0 -> x1, other arithmetic: none -> 0.92 us
    convert_element_type x0 -> x1, local copies, waits for them, and re-layouts: none -> 0.64 us  [fused(): return (both[0].astype(hidden.dtype), both[1].astype(hidden.dtype))]
where the time goes in v3:
time: 60.8 us; the launch traced here: 60.5 us
  Pallas kernels  58.3 us (96%)
  other arithmetic  0.92 us (2%)
  between operations  0.65 us (1%)
  local copies, waits for them, and re-layouts  0.64 us (1%)
    pallas_call x1, Pallas kernels, fused(): pl.pallas_call(functools.partial(step_kernel, pool, tensor), out_shape=bo...  58.3 us

profile of v3, /device:TPU:0, one launch (start us, length us, event | category | flops | bytes accessed | tf_op | source)
XLA Modules:
  0.0 60.5 jit_solution(2372764262845715914)
XLA Ops:
  0.6 58.3 %shard_map.176 = f32[2,2,5120]{2,1,0:T(2,128)} custom-call(bf16[2,5120]{1,0:T(2,128)(2,1)} %hidden_ref.1, f32[1,5120]{1,0:T(1,128)} %bitcast.18, f32[1,128]{1,0:T(1,128)} %bitcast.20, f32[1,128]{1,0:T(1,128)} %bitcast.21, f32[1,5120]{1,0:T(1,128)} %bitcast.19, s32[1,32]{1,0:T(1,128)} %bitcast.22, s32[1,32]{1,0:T(1,128)} %bitcast.23, ...), custom_call_target="tpu_custom_call" | custom-call | tf_op jit(solution)/shard_map/pallas_call | solution.py:727
  59.0 0.9 %convert.4 = bf16[2,2,5120]{2,1,0:T(2,128)(2,1)S(1)} convert(f32[2,2,5120]{2,1,0:T(2,128)} %shard_map.176) | non-fusion elementwise | flops 20480 | bytes 122880 | tf_op jit(solution)/shard_map/convert.1
  59.9 0.6 %slice_bitcast_fusion = (bf16[2,5120]{1,0:T(2,128)(2,1)}, bf16[2,5120]{1,0:T(2,128)(2,1)}) fusion(bf16[2,2,5120]{2,1,0:T(2,128)(2,1)S(1)} %convert.4), kind=kLoop, calls=%fused_computation | loop fusion | bytes 81920 | tf_op jit(solution)/shard_map/convert_element_type | solution.py:747
